TPU v7x, 512 devices: a whole 4x8x8 slice. The times are simulated.
512 devices in a mesh: occ: 8 (over z), vir: 64 (over y, x, core).
Axes of the slice: x: 4, y: 8, z: 8, core: 2. Of those that a mesh axis runs over, the one named last changes fastest.
Arguments:
- amplitudes: bfloat16 [6144, 2048], P('occ', 'vir'), may hold values from -6 to 6
- integrals: bfloat16 [2048, 163840], P('occ', 'vir'), may hold values from -0.375 to 0.375
- occ_sym: int32 [48], P('occ'), may hold values from 0 to 7, as said below
- vir_sym: int32 [1280], P('vir'), may hold values from 0 to 7, as said below
- k_sym: int32 [16], replicated, may hold values from 0 to 7
Outputs:
- ladder: bfloat16 [6144, 163840], P('occ', 'vir')
Inputs may be any that keep to these rules, and one draw needn't show every extreme that they name: `occ_sym`: among the 6 blocks of one index of occ no irrep occurs more than 2 times, and one occurs exactly 2 times. `vir_sym`: among the 20 blocks of one index of vir no irrep occurs more than 5 times, and one occurs exactly 5 times.
All inputs are finite; a program needn't handle non-finite values.
Results may differ from a plain program's by a relative error of at most 0.001.
Values may be sent and summed in bfloat16 or wider, within the bound.
A program may use at most 64 MiB of HBM per device.

v0:
```python
import jax
import jax.numpy as jnp
from jax import lax
from jax.sharding import PartitionSpec as P

BLK = 128
MAXB = 5


def slot_order(symmetry, labels, slot_bound):
    label_count = labels.shape[0]
    positions = jnp.arange(label_count, dtype=jnp.int32)
    matching = labels == symmetry
    ranking = jnp.where(matching, positions, positions + label_count)
    chosen = jnp.argsort(ranking)[:slot_bound]
    return (chosen, matching[chosen])


def slot_table(symmetry, labels, slot_bound):
    chosen, usable = slot_order(symmetry, labels, slot_bound)
    positions = jnp.arange(labels.shape[0], dtype=jnp.int32)
    return ((chosen[:, None] == positions[None, :]) & usable[:, None]).astype(jnp.bfloat16)


def per_device(amplitudes, integrals, occ_sym, vir_sym, k_sym):
    occ_rows = amplitudes.shape[0]
    occ_blocks = occ_rows // BLK
    kblocks = k_sym.shape[0]
    window = kblocks * BLK
    vir_blocks = vir_sym.shape[0]
    col_width = vir_blocks * BLK
    block_ids = jnp.arange(kblocks, dtype=jnp.int32)

    def column_table(symmetry):
        return slot_table(symmetry, vir_sym, MAXB)

    gathered = lax.all_gather(amplitudes, "vir", axis=1, tiled=True)
    allowed = (occ_sym[:, None] == k_sym[None, :]).astype(jnp.bfloat16)
    amp_masked = (
        gathered.reshape(occ_blocks, BLK, kblocks, BLK) * allowed[:, None, :, None]
    ).reshape(occ_rows, window)
    shard_rows = integrals.shape[0]
    own_count = shard_rows // BLK
    first_block = lax.axis_index("occ") * own_count
    own_ids = first_block + jnp.arange(own_count, dtype=jnp.int32)
    own_syms = jnp.sum(jnp.where(own_ids[:, None] == block_ids[None, :], k_sym[None, :], 0), axis=1)
    start_sum = jnp.zeros((occ_rows, vir_blocks, BLK), jnp.float32)
    tables_v = jax.vmap(column_table)(own_syms)
    packed_v = jnp.einsum(
        "bmv,brvc->brmc",
        tables_v,
        integrals.reshape(own_count, BLK, vir_blocks, BLK),
        preferred_element_type=jnp.float32,
    )
    packed_v = packed_v.astype(jnp.bfloat16).reshape(shard_rows, MAXB * BLK)
    shard_piece = lax.all_gather(packed_v, "occ", axis=0, tiled=True)
    piece_blocks = shard_piece.shape[0] // BLK

    def one_block(block_index, running_sum):
        row_start = block_index * BLK
        symmetry = jnp.sum(jnp.where(block_ids == row_start // BLK, k_sym, 0))
        chosen = slot_order(symmetry, vir_sym, MAXB)[0]
        amp_cols = lax.dynamic_slice_in_dim(amp_masked, row_start, BLK, 1)
        block_part = lax.dynamic_slice_in_dim(shard_piece, block_index * BLK, BLK, 0)
        product = jnp.dot(amp_cols, block_part, preferred_element_type=jnp.float32)
        return running_sum.at[:, chosen, :].add(product.reshape(occ_rows, MAXB, BLK))

    summed = lax.fori_loop(0, piece_blocks, one_block, start_sum)
    return summed.reshape(occ_rows, col_width).astype(jnp.bfloat16)


def solution(mesh):
    return jax.shard_map(
        per_device,
        mesh=mesh,
        in_specs=(P("occ", "vir"), P("occ", "vir"), P("occ"), P("vir"), P()),
        out_specs=P("occ", "vir"),
        check_vma=False,
    )
```

profile of v0, /device:TPU:4, one launch (start us, length us, event | category | flops | bytes accessed | tf_op | source)
XLA Modules:
  0.0 402.5 jit_solution(3272119504203592197)
XLA Ops:
  10.9 2.6 reshape.82
  15.0 82.5 %all-gather.3.cloned.1.call-done = bf16[768,2048]{0,1:T(8,128)(2,1)} async-done(((bf16[768,32]{0,1:T(8,128)(2,1)}), bf16[768,2048]{0,1:T(8,128)(2,1)}) %all-gather.3.cloned.1.call-update) | async-done | bytes 3145744 | tf_op jit(solution)/shard_map/all_gather | solution.py:37
  97.5 3.2 copy.43
  101.2 2.4 bitcast_multiply_fusion
  103.5 49.2 %all-gather.5.cloned.1.call-done = bf16[2048,640]{0,1:T(8,128)(2,1)} async-done(((bf16[256,640]{0,1:T(8,128)(2,1)}), bf16[2048,640]{0,1:T(8,128)(2,1)}) %all-gather.5.cloned.1.call-update) | async-done | bytes 2621456 | tf_op jit(solution)/shard_map/all_gather | solution.py:56
  152.7 3.9 broadcast_in_dim.62
  156.6 225.5 %while.16 = (s32[]{:T(128)}, f32[768,20,128]{2,0,1:T(8,128)}, s32[16]{0:T(128)S(1)}, s32[20]{0:T(128)S(1)}, bf16[768,2048]{1,0:T(8,128)(2,1)}, /*index=5*/bf16[2...) while((s32[]{:T(128)}, f32[768,20,128]{2,0,1:T(8,128)}, ...), condition=%wide.region_6.7_spmd.clone, body=%wide.region_2.6_spmd.clone.sunk | while | flops 126320880 | bytes 12158960 | solution.py:68
  158.0 1.7 sort.51
  159.7 2.7 fusion.23
  162.4 1.9 copy.63
  164.3 6.4 %scatter_fusion = f32[768,20,128]{2,0,1:T(8,128)} fusion(f32[768,20,128]{2,0,1:T(8,128)} %get-tuple-element.294, s32[5]{0:T(128)S(1)} %compare_select_fusion.8, f32[5,768,128]{2,1,0:T(8,128)S(1)} %bitcast.27), kind=kCustom, calls=%fused_computation.1.clone.clone.1 | custom fusion | flops 491520 | bytes 5898260 | tf_op jit(solution)/shard_map/while/body/eval_jaxpr/scatter-add | solution.py:66
  172.1 1.7 sort.51
  173.8 2.7 fusion.23
  176.4 1.9 copy.63
  178.3 6.4 %scatter_fusion = f32[768,20,128]{2,0,1:T(8,128)} fusion(f32[768,20,128]{2,0,1:T(8,128)} %get-tuple-element.294, s32[5]{0:T(128)S(1)} %compare_select_fusion.8, f32[5,768,128]{2,1,0:T(8,128)S(1)} %bitcast.27), kind=kCustom, calls=%fused_computation.1.clone.clone.1 | custom fusion | flops 491520 | bytes 5898260 | tf_op jit(solution)/shard_map/while/body/eval_jaxpr/scatter-add | solution.py:66
  187.8 2.7 fusion.23
  190.5 1.9 copy.63
  192.4 6.4 %scatter_fusion = f32[768,20,128]{2,0,1:T(8,128)} fusion(f32[768,20,128]{2,0,1:T(8,128)} %get-tuple-element.294, s32[5]{0:T(128)S(1)} %compare_select_fusion.8, f32[5,768,128]{2,1,0:T(8,128)S(1)} %bitcast.27), kind=kCustom, calls=%fused_computation.1.clone.clone.1 | custom fusion | flops 491520 | bytes 5898260 | tf_op jit(solution)/shard_map/while/body/eval_jaxpr/scatter-add | solution.py:66
  200.2 1.7 sort.51
  201.9 2.7 fusion.23
  204.6 1.9 copy.63
  206.5 6.4 %scatter_fusion = f32[768,20,128]{2,0,1:T(8,128)} fusion(f32[768,20,128]{2,0,1:T(8,128)} %get-tuple-element.294, s32[5]{0:T(128)S(1)} %compare_select_fusion.8, f32[5,768,128]{2,1,0:T(8,128)S(1)} %bitcast.27), kind=kCustom, calls=%fused_computation.1.clone.clone.1 | custom fusion | flops 491520 | bytes 5898260 | tf_op jit(solution)/shard_map/while/body/eval_jaxpr/scatter-add | solution.py:66
  214.3 1.7 sort.51
  216.0 2.7 fusion.23
  218.7 1.9 copy.63
  220.6 6.4 %scatter_fusion = f32[768,20,128]{2,0,1:T(8,128)} fusion(f32[768,20,128]{2,0,1:T(8,128)} %get-tuple-element.294, s32[5]{0:T(128)S(1)} %compare_select_fusion.8, f32[5,768,128]{2,1,0:T(8,128)S(1)} %bitcast.27), kind=kCustom, calls=%fused_computation.1.clone.clone.1 | custom fusion | flops 491520 | bytes 5898260 | tf_op jit(solution)/shard_map/while/body/eval_jaxpr/scatter-add | solution.py:66
  230.1 2.7 fusion.23
  232.7 1.9 copy.63
  234.6 6.4 %scatter_fusion = f32[768,20,128]{2,0,1:T(8,128)} fusion(f32[768,20,128]{2,0,1:T(8,128)} %get-tuple-element.294, s32[5]{0:T(128)S(1)} %compare_select_fusion.8, f32[5,768,128]{2,1,0:T(8,128)S(1)} %bitcast.27), kind=kCustom, calls=%fused_computation.1.clone.clone.1 | custom fusion | flops 491520 | bytes 5898260 | tf_op jit(solution)/shard_map/while/body/eval_jaxpr/scatter-add | solution.py:66
  242.5 1.7 sort.51
  244.1 2.7 fusion.23
  246.8 1.9 copy.63
  248.7 6.5 %scatter_fusion = f32[768,20,128]{2,0,1:T(8,128)} fusion(f32[768,20,128]{2,0,1:T(8,128)} %get-tuple-element.294, s32[5]{0:T(128)S(1)} %compare_select_fusion.8, f32[5,768,128]{2,1,0:T(8,128)S(1)} %bitcast.27), kind=kCustom, calls=%fused_computation.1.clone.clone.1 | custom fusion | flops 491520 | bytes 5898260 | tf_op jit(solution)/shard_map/while/body/eval_jaxpr/scatter-add | solution.py:66
  258.3 2.7 fusion.23
  261.0 1.9 copy.63
  262.8 6.4 %scatter_fusion = f32[768,20,128]{2,0,1:T(8,128)} fusion(f32[768,20,128]{2,0,1:T(8,128)} %get-tuple-element.294, s32[5]{0:T(128)S(1)} %compare_select_fusion.8, f32[5,768,128]{2,1,0:T(8,128)S(1)} %bitcast.27), kind=kCustom, calls=%fused_computation.1.clone.clone.1 | custom fusion | flops 491520 | bytes 5898260 | tf_op jit(solution)/shard_map/while/body/eval_jaxpr/scatter-add | solution.py:66
  270.7 1.7 sort.51
  272.3 2.7 fusion.23
  275.0 1.9 copy.63
  276.9 6.4 %scatter_fusion = f32[768,20,128]{2,0,1:T(8,128)} fusion(f32[768,20,128]{2,0,1:T(8,128)} %get-tuple-element.294, s32[5]{0:T(128)S(1)} %compare_select_fusion.8, f32[5,768,128]{2,1,0:T(8,128)S(1)} %bitcast.27), kind=kCustom, calls=%fused_computation.1.clone.clone.1 | custom fusion | flops 491520 | bytes 5898260 | tf_op jit(solution)/shard_map/while/body/eval_jaxpr/scatter-add | solution.py:66
  286.4 2.7 fusion.23
  289.1 1.9 copy.63
  291.0 6.5 %scatter_fusion = f32[768,20,128]{2,0,1:T(8,128)} fusion(f32[768,20,128]{2,0,1:T(8,128)} %get-tuple-element.294, s32[5]{0:T(128)S(1)} %compare_select_fusion.8, f32[5,768,128]{2,1,0:T(8,128)S(1)} %bitcast.27), kind=kCustom, calls=%fused_computation.1.clone.clone.1 | custom fusion | flops 491520 | bytes 5898260 | tf_op jit(solution)/shard_map/while/body/eval_jaxpr/scatter-add | solution.py:66
  300.6 2.7 fusion.23
  303.3 1.9 copy.63
  305.2 6.4 %scatter_fusion = f32[768,20,128]{2,0,1:T(8,128)} fusion(f32[768,20,128]{2,0,1:T(8,128)} %get-tuple-element.294, s32[5]{0:T(128)S(1)} %compare_select_fusion.8, f32[5,768,128]{2,1,0:T(8,128)S(1)} %bitcast.27), kind=kCustom, calls=%fused_computation.1.clone.clone.1 | custom fusion | flops 491520 | bytes 5898260 | tf_op jit(solution)/shard_map/while/body/eval_jaxpr/scatter-add | solution.py:66
  313.0 1.7 sort.51
  314.6 2.7 fusion.23
  317.3 1.9 copy.63
  319.2 6.5 %scatter_fusion = f32[768,20,128]{2,0,1:T(8,128)} fusion(f32[768,20,128]{2,0,1:T(8,128)} %get-tuple-element.294, s32[5]{0:T(128)S(1)} %compare_select_fusion.8, f32[5,768,128]{2,1,0:T(8,128)S(1)} %bitcast.27), kind=kCustom, calls=%fused_computation.1.clone.clone.1 | custom fusion | flops 491520 | bytes 5898260 | tf_op jit(solution)/shard_map/while/body/eval_jaxpr/scatter-add | solution.py:66
  328.7 2.7 fusion.23
  331.4 1.9 copy.63
  333.3 6.5 %scatter_fusion = f32[768,20,128]{2,0,1:T(8,128)} fusion(f32[768,20,128]{2,0,1:T(8,128)} %get-tuple-element.294, s32[5]{0:T(128)S(1)} %compare_select_fusion.8, f32[5,768,128]{2,1,0:T(8,128)S(1)} %bitcast.27), kind=kCustom, calls=%fused_computation.1.clone.clone.1 | custom fusion | flops 491520 | bytes 5898260 | tf_op jit(solution)/shard_map/while/body/eval_jaxpr/scatter-add | solution.py:66
  342.9 2.7 fusion.23
  345.6 1.9 copy.63
  347.5 6.5 %scatter_fusion = f32[768,20,128]{2,0,1:T(8,128)} fusion(f32[768,20,128]{2,0,1:T(8,128)} %get-tuple-element.294, s32[5]{0:T(128)S(1)} %compare_select_fusion.8, f32[5,768,128]{2,1,0:T(8,128)S(1)} %bitcast.27), kind=kCustom, calls=%fused_computation.1.clone.clone.1 | custom fusion | flops 491520 | bytes 5898260 | tf_op jit(solution)/shard_map/while/body/eval_jaxpr/scatter-add | solution.py:66
  357.0 2.7 fusion.23
  359.7 1.9 copy.63
  361.6 6.4 %scatter_fusion = f32[768,20,128]{2,0,1:T(8,128)} fusion(f32[768,20,128]{2,0,1:T(8,128)} %get-tuple-element.294, s32[5]{0:T(128)S(1)} %compare_select_fusion.8, f32[5,768,128]{2,1,0:T(8,128)S(1)} %bitcast.27), kind=kCustom, calls=%fused_computation.1.clone.clone.1 | custom fusion | flops 491520 | bytes 5898260 | tf_op jit(solution)/shard_map/while/body/eval_jaxpr/scatter-add | solution.py:66
  371.1 2.7 fusion.23
  373.8 1.9 copy.63
  375.7 6.5 %scatter_fusion = f32[768,20,128]{2,0,1:T(8,128)} fusion(f32[768,20,128]{2,0,1:T(8,128)} %get-tuple-element.294, s32[5]{0:T(128)S(1)} %compare_select_fusion.8, f32[5,768,128]{2,1,0:T(8,128)S(1)} %bitcast.27), kind=kCustom, calls=%fused_computation.1.clone.clone.1 | custom fusion | flops 491520 | bytes 5898260 | tf_op jit(solution)/shard_map/while/body/eval_jaxpr/scatter-add | solution.py:66
  382.2 7.2 %copy.51 = bf16[768,20,128]{0,2,1:T(8,128)(2,1)} copy(f32[768,20,128]{2,0,1:T(8,128)} %get-tuple-element.185) | data formatting | bytes 11796480 | tf_op jit(solution)/shard_map/while | solution.py:68
  389.4 6.3 %copy.52 = bf16[768,2560]{1,0:T(8,128)(2,1)} copy(bf16[768,2560]{0,1:T(8,128)(2,1)} %bitcast.29) | data formatting | bytes 7864320 | tf_op jit(solution)/shard_map/convert_element_type | solution.py:69
  (102 shorter events, 43.2 us)
Async XLA Ops:
  6.5 90.9 %all-gather.3.cloned.1.call-start = ((), (), s32[]{:S(2)}) async-start(), calls=%async_computation | async-start | bytes 3194880 | tf_op jit(solution)/shard_map/all_gather | solution.py:37
  7.3 145.4 %all-gather.5.cloned.1.call-start = ((), (), s32[]{:S(2)}) async-start(), calls=%async_computation.1 | async-start | bytes 2949120 | tf_op jit(solution)/shard_map/all_gather | solution.py:56
  10.9 4.0 copy-start
  10.9 4.0 copy-start.1
  103.5 53.1 %copy-start.2 = (s32[20]{0:T(128)S(1)}, s32[20]{0:T(128)}, u32[]{:S(2)}) copy-start(s32[20]{0:T(128)} %param.10) | copy-start | bytes 244
Sparse Core Ops, SparseCore 0:
  10.7 86.7 all-gather.2
  99.5 53.1 all-gather.4
where the time goes:
time: 405 us; the launch traced here: 402 us
  other arithmetic  157 us (39%)
  waiting for transfers between devices  132 us (33%)
  local copies, waits for them, and re-layouts  56 us (14%)
  matrix products  43.5 us (11%)
  between operations  13.5 us (3%)
    scatter-add x16, other arithmetic, one_block(): running_sum.at[:, chosen, :].add(product.reshape(occ_rows, MAXB, BLK))  103 us
    all_gather x1, waiting for transfers between devices, per_device(): gathered = lax.all_gather(amplitudes, 'vir', axis=1, tiled=True)  82.5 us
    all_gather x1, waiting for transfers between devices, per_device(): shard_piece = lax.all_gather(packed_v, 'occ', axis=0, tiled=True)  49.2 us
    dot_general x16, matrix products, one_block(): product = jnp.dot(amp_cols, block_part, preferred_element_type=jnp.float32)  43 us
    reshape x16, local copies, waits for them, and re-layouts, one_block(): product.reshape(occ_rows, MAXB, BLK)  30.2 us
    sort x17, other arithmetic, slot_order(): chosen = jnp.argsort(ranking)[:slot_bound]  27.5 us
    select_n x17, other arithmetic, slot_order(): ranking = jnp.where(matching, positions, positions + label_count)  11.5 us
    reduce_sum x16, other arithmetic, one_block(): symmetry = jnp.sum(jnp.where(block_ids == row_start // BLK, k_sym, 0))  11.1 us
  transfers between devices with their start and end apart: 2, of which 2 were waited for; matrix products, arithmetic and copies ran while one was open for 3% of the time, Pallas kernels for 0%

commit v1 on v0

--- a/solution.py
+++ b/solution.py
@@ -53,7 +53,25 @@
         preferred_element_type=jnp.float32,
     )
     packed_v = packed_v.astype(jnp.bfloat16).reshape(shard_rows, MAXB * BLK)
-    shard_piece = lax.all_gather(packed_v, "occ", axis=0, tiled=True)
+
+    def save_bars(state):
+        bus_axis = "occ"
+        shares = lax.axis_size(bus_axis)
+        aux = list(map(lambda c: (c - 1, c), range(1, shares))) + [(shares - 1, 0)]
+        k_now = state
+        leaves = [k_now]
+        i0 = 0
+        while i0 < shares - 1:
+            k_now = lax.ppermute(k_now, bus_axis, aux)
+            leaves += [k_now]
+            i0 = i0 + 1
+        return jnp.roll(
+            jnp.concatenate([*reversed(leaves)], axis=0),
+            (lax.axis_index(bus_axis) + 1) * k_now.shape[0],
+            axis=0,
+        )
+
+    shard_piece = save_bars(packed_v)
     piece_blocks = shard_piece.shape[0] // BLK
 
     def one_block(block_index, running_sum):

time: 405 us -> 358 us (0.88)
  the two profiles are of different devices: /device:TPU:4 before, /device:TPU:1 now
where the time goes in v1:
time: 358 us; the launch traced here: 356 us
  other arithmetic  156 us (44%)
  waiting for transfers between devices  67.7 us (19%)
  local copies, waits for them, and re-layouts  57.7 us (16%)
  matrix products  43.5 us (12%)
  starting transfers between devices  16.3 us (5%)
  between operations  13.7 us (4%)
    scatter-add x16, other arithmetic, one_block(): running_sum.at[:, chosen, :].add(product.reshape(occ_rows, MAXB, BLK))  103 us
    ppermute x7, waiting for transfers between devices, save_bars(): k_now = lax.ppermute(k_now, bus_axis, aux)  60.6 us
    dot_general x16, matrix products, one_block(): product = jnp.dot(amp_cols, block_part, preferred_element_type=jnp.float32)  43.1 us
    reshape x16, local copies, waits for them, and re-layouts, one_block(): product.reshape(occ_rows, MAXB, BLK)  30.2 us
    sort x17, other arithmetic, slot_order(): chosen = jnp.argsort(ranking)[:slot_bound]  27.5 us
    ppermute x7, starting transfers between devices, save_bars(): k_now = lax.ppermute(k_now, bus_axis, aux)  16.3 us
    select_n x17, other arithmetic, slot_order(): ranking = jnp.where(matching, positions, positions + label_count)  11.5 us
    reduce_sum x16, other arithmetic, one_block(): symmetry = jnp.sum(jnp.where(block_ids == row_start // BLK, k_sym, 0))  11.1 us
  transfers between devices with their start and end apart: 8, of which 8 were waited for; matrix products, arithmetic and copies ran while one was open for 3% of the time, Pallas kernels for 0%

profile of v1, /device:TPU:1, one launch (start us, length us, event | category | flops | bytes accessed | tf_op | source)
XLA Modules:
  0.0 355.8 jit_solution(4775144679956810076)
XLA Ops:
  10.9 2.5 reshape.82
  14.1 4.8 %collective-permute-start = (bf16[256,640]{0,1:T(8,128)(2,1)S(1)}, bf16[256,640]{0,1:T(8,128)(2,1)S(1)}, u32[]{:S(2)}, u32[]{:S(2)}) collective-permute-start(bf16[256,640]{0,1:T(8,128)(2,1)S(1)} %copy.55), channel_id=1, source_target_pairs={{0,64},{64,128},{128,192},{192,256},{256,320},{320,384},{384,448},... | collective-permute-start | bytes 983048 | tf_op jit(solution)/shard_map/ppermute | solution.py:65
  18.9 14.1 %collective-permute-done = bf16[256,640]{0,1:T(8,128)(2,1)S(1)} collective-permute-done((bf16[256,640]{0,1:T(8,128)(2,1)S(1)}, bf16[256,640]{0,1:T(8,128)(2,1)S(1)}, u32[]{:S(2)}, u32[]{:S(2)}) %collective-permute-start) | collective-permute-done | bytes 327712 | tf_op jit(solution)/shard_map/ppermute | solution.py:65
  33.0 1.9 collective-permute-start.1
  34.9 9.2 %collective-permute-done.1 = bf16[256,640]{0,1:T(8,128)(2,1)S(1)} collective-permute-done((bf16[256,640]{0,1:T(8,128)(2,1)S(1)}, bf16[256,640]{0,1:T(8,128)(2,1)S(1)}, u32[]{:S(2)}, u32[]{:S(2)}) %collective-permute-start.1) | collective-permute-done | bytes 327712 | tf_op jit(solution)/shard_map/ppermute | solution.py:65
  44.1 1.9 collective-permute-start.2
  46.0 8.4 %collective-permute-done.2 = bf16[256,640]{0,1:T(8,128)(2,1)S(1)} collective-permute-done((bf16[256,640]{0,1:T(8,128)(2,1)S(1)}, bf16[256,640]{0,1:T(8,128)(2,1)S(1)}, u32[]{:S(2)}, u32[]{:S(2)}) %collective-permute-start.2) | collective-permute-done | bytes 327712 | tf_op jit(solution)/shard_map/ppermute | solution.py:65
  54.4 1.9 collective-permute-start.3
  56.3 7.5 %collective-permute-done.3 = bf16[256,640]{0,1:T(8,128)(2,1)S(1)} collective-permute-done((bf16[256,640]{0,1:T(8,128)(2,1)S(1)}, bf16[256,640]{0,1:T(8,128)(2,1)S(1)}, u32[]{:S(2)}, u32[]{:S(2)}) %collective-permute-start.3) | collective-permute-done | bytes 327712 | tf_op jit(solution)/shard_map/ppermute | solution.py:65
  63.8 1.9 collective-permute-start.4
  65.7 7.1 %collective-permute-done.4 = bf16[256,640]{0,1:T(8,128)(2,1)S(1)} collective-permute-done((bf16[256,640]{0,1:T(8,128)(2,1)S(1)}, bf16[256,640]{0,1:T(8,128)(2,1)S(1)}, u32[]{:S(2)}, u32[]{:S(2)}) %collective-permute-start.4) | collective-permute-done | bytes 327712 | tf_op jit(solution)/shard_map/ppermute | solution.py:65
  72.8 1.9 collective-permute-start.5
  74.7 7.1 %collective-permute-done.5 = bf16[256,640]{0,1:T(8,128)(2,1)S(1)} collective-permute-done((bf16[256,640]{0,1:T(8,128)(2,1)S(1)}, bf16[256,640]{0,1:T(8,128)(2,1)S(1)}, u32[]{:S(2)}, u32[]{:S(2)}) %collective-permute-start.5) | collective-permute-done | bytes 327712 | tf_op jit(solution)/shard_map/ppermute | solution.py:65
  81.9 1.9 collective-permute-start.6
  83.9 7.2 %collective-permute-done.6 = bf16[256,640]{0,1:T(8,128)(2,1)S(1)} collective-permute-done((bf16[256,640]{0,1:T(8,128)(2,1)S(1)}, bf16[256,640]{0,1:T(8,128)(2,1)S(1)}, u32[]{:S(2)}, u32[]{:S(2)}) %collective-permute-start.6) | collective-permute-done | bytes 327712 | tf_op jit(solution)/shard_map/ppermute | solution.py:65
  91.9 1.9 constant_dynamic-slice_fusion
  93.8 6.4 %all-gather.2.cloned.1.call-done = bf16[768,2048]{0,1:T(8,128)(2,1)} async-done(((bf16[768,32]{0,1:T(8,128)(2,1)}), bf16[768,2048]{0,1:T(8,128)(2,1)}) %all-gather.2.cloned.1.call-update) | async-done | bytes 3145744 | tf_op jit(solution)/shard_map/all_gather | solution.py:37
  100.2 3.2 copy.43
  103.8 2.4 bitcast_multiply_fusion
  106.2 3.9 %broadcast_in_dim.62 = f32[768,20,128]{2,0,1:T(8,128)} broadcast(f32[]{:T(128)} %constant.114.clone.1), dimensions={} | broadcast | bytes 7864324 | tf_op jit(solution)/shard_map/broadcast_in_dim | solution.py:47
  110.1 225.3 %while.16 = (s32[]{:T(128)}, f32[768,20,128]{2,0,1:T(8,128)}, s32[16]{0:T(128)S(1)}, s32[20]{0:T(128)S(1)}, bf16[768,2048]{1,0:T(8,128)(2,1)}, /*index=5*/bf16[2...) while((s32[]{:T(128)}, f32[768,20,128]{2,0,1:T(8,128)}, ...), condition=%wide.region_6.7_spmd.clone, body=%wide.region_2.6_spmd.clone.sunk | while | flops 126320880 | bytes 12158960 | solution.py:86
  113.2 2.7 fusion.23
  115.9 1.9 copy.63
  117.8 6.5 %scatter_fusion = f32[768,20,128]{2,0,1:T(8,128)} fusion(f32[768,20,128]{2,0,1:T(8,128)} %get-tuple-element.294, s32[5]{0:T(128)S(1)} %compare_select_fusion.8, f32[5,768,128]{2,1,0:T(8,128)S(1)} %bitcast.27), kind=kCustom, calls=%fused_computation.1.clone.clone.1 | custom fusion | flops 491520 | bytes 5898260 | tf_op jit(solution)/shard_map/while/body/eval_jaxpr/scatter-add | solution.py:84
  127.3 2.7 fusion.23
  130.0 1.9 copy.63
  131.9 6.4 %scatter_fusion = f32[768,20,128]{2,0,1:T(8,128)} fusion(f32[768,20,128]{2,0,1:T(8,128)} %get-tuple-element.294, s32[5]{0:T(128)S(1)} %compare_select_fusion.8, f32[5,768,128]{2,1,0:T(8,128)S(1)} %bitcast.27), kind=kCustom, calls=%fused_computation.1.clone.clone.1 | custom fusion | flops 491520 | bytes 5898260 | tf_op jit(solution)/shard_map/while/body/eval_jaxpr/scatter-add | solution.py:84
  141.4 2.7 fusion.23
  144.1 1.9 copy.63
  146.0 6.5 %scatter_fusion = f32[768,20,128]{2,0,1:T(8,128)} fusion(f32[768,20,128]{2,0,1:T(8,128)} %get-tuple-element.294, s32[5]{0:T(128)S(1)} %compare_select_fusion.8, f32[5,768,128]{2,1,0:T(8,128)S(1)} %bitcast.27), kind=kCustom, calls=%fused_computation.1.clone.clone.1 | custom fusion | flops 491520 | bytes 5898260 | tf_op jit(solution)/shard_map/while/body/eval_jaxpr/scatter-add | solution.py:84
  155.5 2.7 fusion.23
  158.2 1.9 copy.63
  160.1 6.4 %scatter_fusion = f32[768,20,128]{2,0,1:T(8,128)} fusion(f32[768,20,128]{2,0,1:T(8,128)} %get-tuple-element.294, s32[5]{0:T(128)S(1)} %compare_select_fusion.8, f32[5,768,128]{2,1,0:T(8,128)S(1)} %bitcast.27), kind=kCustom, calls=%fused_computation.1.clone.clone.1 | custom fusion | flops 491520 | bytes 5898260 | tf_op jit(solution)/shard_map/while/body/eval_jaxpr/scatter-add | solution.py:84
  169.6 2.7 fusion.23
  172.3 1.9 copy.63
  174.2 6.4 %scatter_fusion = f32[768,20,128]{2,0,1:T(8,128)} fusion(f32[768,20,128]{2,0,1:T(8,128)} %get-tuple-element.294, s32[5]{0:T(128)S(1)} %compare_select_fusion.8, f32[5,768,128]{2,1,0:T(8,128)S(1)} %bitcast.27), kind=kCustom, calls=%fused_computation.1.clone.clone.1 | custom fusion | flops 491520 | bytes 5898260 | tf_op jit(solution)/shard_map/while/body/eval_jaxpr/scatter-add | solution.py:84
  183.7 2.7 fusion.23
  186.4 1.9 copy.63
  188.3 6.4 %scatter_fusion = f32[768,20,128]{2,0,1:T(8,128)} fusion(f32[768,20,128]{2,0,1:T(8,128)} %get-tuple-element.294, s32[5]{0:T(128)S(1)} %compare_select_fusion.8, f32[5,768,128]{2,1,0:T(8,128)S(1)} %bitcast.27), kind=kCustom, calls=%fused_computation.1.clone.clone.1 | custom fusion | flops 491520 | bytes 5898260 | tf_op jit(solution)/shard_map/while/body/eval_jaxpr/scatter-add | solution.py:84
  197.8 2.7 fusion.23
  200.4 1.9 copy.63
  202.3 6.4 %scatter_fusion = f32[768,20,128]{2,0,1:T(8,128)} fusion(f32[768,20,128]{2,0,1:T(8,128)} %get-tuple-element.294, s32[5]{0:T(128)S(1)} %compare_select_fusion.8, f32[5,768,128]{2,1,0:T(8,128)S(1)} %bitcast.27), kind=kCustom, calls=%fused_computation.1.clone.clone.1 | custom fusion | flops 491520 | bytes 5898260 | tf_op jit(solution)/shard_map/while/body/eval_jaxpr/scatter-add | solution.py:84
  211.8 2.7 fusion.23
  214.5 1.9 copy.63
  216.4 6.4 %scatter_fusion = f32[768,20,128]{2,0,1:T(8,128)} fusion(f32[768,20,128]{2,0,1:T(8,128)} %get-tuple-element.294, s32[5]{0:T(128)S(1)} %compare_select_fusion.8, f32[5,768,128]{2,1,0:T(8,128)S(1)} %bitcast.27), kind=kCustom, calls=%fused_computation.1.clone.clone.1 | custom fusion | flops 491520 | bytes 5898260 | tf_op jit(solution)/shard_map/while/body/eval_jaxpr/scatter-add | solution.py:84
  225.9 2.7 fusion.23
  228.6 1.9 copy.63
  230.5 6.4 %scatter_fusion = f32[768,20,128]{2,0,1:T(8,128)} fusion(f32[768,20,128]{2,0,1:T(8,128)} %get-tuple-element.294, s32[5]{0:T(128)S(1)} %compare_select_fusion.8, f32[5,768,128]{2,1,0:T(8,128)S(1)} %bitcast.27), kind=kCustom, calls=%fused_computation.1.clone.clone.1 | custom fusion | flops 491520 | bytes 5898260 | tf_op jit(solution)/shard_map/while/body/eval_jaxpr/scatter-add | solution.py:84
  240.0 2.7 fusion.23
  244.6 6.4 %scatter_fusion = f32[768,20,128]{2,0,1:T(8,128)} fusion(f32[768,20,128]{2,0,1:T(8,128)} %get-tuple-element.294, s32[5]{0:T(128)S(1)} %compare_select_fusion.8, f32[5,768,128]{2,1,0:T(8,128)S(1)} %bitcast.27), kind=kCustom, calls=%fused_computation.1.clone.clone.1 | custom fusion | flops 491520 | bytes 5898260 | tf_op jit(solution)/shard_map/while/body/eval_jaxpr/scatter-add | solution.py:84
  254.0 2.7 fusion.23
  258.6 6.4 %scatter_fusion = f32[768,20,128]{2,0,1:T(8,128)} fusion(f32[768,20,128]{2,0,1:T(8,128)} %get-tuple-element.294, s32[5]{0:T(128)S(1)} %compare_select_fusion.8, f32[5,768,128]{2,1,0:T(8,128)S(1)} %bitcast.27), kind=kCustom, calls=%fused_computation.1.clone.clone.1 | custom fusion | flops 491520 | bytes 5898260 | tf_op jit(solution)/shard_map/while/body/eval_jaxpr/scatter-add | solution.py:84
  268.1 2.7 fusion.23
  272.7 6.4 %scatter_fusion = f32[768,20,128]{2,0,1:T(8,128)} fusion(f32[768,20,128]{2,0,1:T(8,128)} %get-tuple-element.294, s32[5]{0:T(128)S(1)} %compare_select_fusion.8, f32[5,768,128]{2,1,0:T(8,128)S(1)} %bitcast.27), kind=kCustom, calls=%fused_computation.1.clone.clone.1 | custom fusion | flops 491520 | bytes 5898260 | tf_op jit(solution)/shard_map/while/body/eval_jaxpr/scatter-add | solution.py:84
  282.2 2.7 fusion.23
  286.8 6.4 %scatter_fusion = f32[768,20,128]{2,0,1:T(8,128)} fusion(f32[768,20,128]{2,0,1:T(8,128)} %get-tuple-element.294, s32[5]{0:T(128)S(1)} %compare_select_fusion.8, f32[5,768,128]{2,1,0:T(8,128)S(1)} %bitcast.27), kind=kCustom, calls=%fused_computation.1.clone.clone.1 | custom fusion | flops 491520 | bytes 5898260 | tf_op jit(solution)/shard_map/while/body/eval_jaxpr/scatter-add | solution.py:84
  296.2 2.7 fusion.23
  300.8 6.5 %scatter_fusion = f32[768,20,128]{2,0,1:T(8,128)} fusion(f32[768,20,128]{2,0,1:T(8,128)} %get-tuple-element.294, s32[5]{0:T(128)S(1)} %compare_select_fusion.8, f32[5,768,128]{2,1,0:T(8,128)S(1)} %bitcast.27), kind=kCustom, calls=%fused_computation.1.clone.clone.1 | custom fusion | flops 491520 | bytes 5898260 | tf_op jit(solution)/shard_map/while/body/eval_jaxpr/scatter-add | solution.py:84
  310.4 2.7 fusion.23
  315.0 6.4 %scatter_fusion = f32[768,20,128]{2,0,1:T(8,128)} fusion(f32[768,20,128]{2,0,1:T(8,128)} %get-tuple-element.294, s32[5]{0:T(128)S(1)} %compare_select_fusion.8, f32[5,768,128]{2,1,0:T(8,128)S(1)} %bitcast.27), kind=kCustom, calls=%fused_computation.1.clone.clone.1 | custom fusion | flops 491520 | bytes 5898260 | tf_op jit(solution)/shard_map/while/body/eval_jaxpr/scatter-add | solution.py:84
  324.4 2.7 fusion.23
  329.0 6.4 %scatter_fusion = f32[768,20,128]{2,0,1:T(8,128)} fusion(f32[768,20,128]{2,0,1:T(8,128)} %get-tuple-element.294, s32[5]{0:T(128)S(1)} %compare_select_fusion.8, f32[5,768,128]{2,1,0:T(8,128)S(1)} %bitcast.27), kind=kCustom, calls=%fused_computation.1.clone.clone.1 | custom fusion | flops 491520 | bytes 5898260 | tf_op jit(solution)/shard_map/while/body/eval_jaxpr/scatter-add | solution.py:84
  335.4 7.2 %copy.51 = bf16[768,20,128]{0,2,1:T(8,128)(2,1)} copy(f32[768,20,128]{2,0,1:T(8,128)} %get-tuple-element.185) | data formatting | bytes 11796480 | tf_op jit(solution)/shard_map/while | solution.py:86
  342.6 6.3 %copy.52 = bf16[768,2560]{1,0:T(8,128)(2,1)} copy(bf16[768,2560]{0,1:T(8,128)(2,1)} %bitcast.29) | data formatting | bytes 7864320 | tf_op jit(solution)/shard_map/convert_element_type | solution.py:87
  (130 shorter events, 67.9 us)
Async XLA Ops:
  6.5 77.3 %copy-start.1 = (s32[16]{0:T(128)S(1)}, s32[16]{0:T(128)}, u32[]{:S(2)}) copy-start(s32[16]{0:T(128)} %param.11) | copy-start | bytes 196
  6.5 77.3 %copy-start = (s32[6]{0:T(128)S(1)}, s32[6]{0:T(128)}, u32[]{:S(2)}) copy-start(s32[6]{0:T(128)} %param.9) | copy-start | bytes 76
  6.5 93.6 %all-gather.2.cloned.1.call-start = ((), (), s32[]{:S(2)}) async-start(), calls=%async_computation | async-start | bytes 3194880 | tf_op jit(solution)/shard_map/all_gather | solution.py:37
  14.1 18.9 %collective-permute-start = (bf16[256,640]{0,1:T(8,128)(2,1)S(1)}, bf16[256,640]{0,1:T(8,128)(2,1)S(1)}, u32[]{:S(2)}, u32[]{:S(2)}) collective-permute-start(bf16[256,640]{0,1:T(8,128)(2,1)S(1)} %copy.55), channel_id=1, source_target_pairs={{0,64},{64,128},{128,192},{192,256},{256,320},{320,384},{384,448},... | collective-permute-start | bytes 983048 | tf_op jit(solution)/shard_map/ppermute | solution.py:65
  33.0 11.1 %collective-permute-start.1 = (bf16[256,640]{0,1:T(8,128)(2,1)S(1)}, bf16[256,640]{0,1:T(8,128)(2,1)S(1)}, u32[]{:S(2)}, u32[]{:S(2)}) collective-permute-start(bf16[256,640]{0,1:T(8,128)(2,1)S(1)} %collective-permute-done), channel_id=1, source_target_pairs={{0,64},{64,128},{128,192},{192,256},{256,320},{320,384},{384,448},... | collective-permute-start | bytes 983048 | tf_op jit(solution)/shard_map/ppermute | solution.py:65
  44.1 10.3 %collective-permute-start.2 = (bf16[256,640]{0,1:T(8,128)(2,1)S(1)}, bf16[256,640]{0,1:T(8,128)(2,1)S(1)}, u32[]{:S(2)}, u32[]{:S(2)}) collective-permute-start(bf16[256,640]{0,1:T(8,128)(2,1)S(1)} %collective-permute-done.1), channel_id=1, source_target_pairs={{0,64},{64,128},{128,192},{192,256},{256,320},{320,384},{384,448},... | collective-permute-start | bytes 983048 | tf_op jit(solution)/shard_map/ppermute | solution.py:65
  54.4 9.4 %collective-permute-start.3 = (bf16[256,640]{0,1:T(8,128)(2,1)S(1)}, bf16[256,640]{0,1:T(8,128)(2,1)S(1)}, u32[]{:S(2)}, u32[]{:S(2)}) collective-permute-start(bf16[256,640]{0,1:T(8,128)(2,1)S(1)} %collective-permute-done.2), channel_id=1, source_target_pairs={{0,64},{64,128},{128,192},{192,256},{256,320},{320,384},{384,448},... | collective-permute-start | bytes 983048 | tf_op jit(solution)/shard_map/ppermute | solution.py:65
  63.8 9.0 %collective-permute-start.4 = (bf16[256,640]{0,1:T(8,128)(2,1)S(1)}, bf16[256,640]{0,1:T(8,128)(2,1)S(1)}, u32[]{:S(2)}, u32[]{:S(2)}) collective-permute-start(bf16[256,640]{0,1:T(8,128)(2,1)S(1)} %collective-permute-done.3), channel_id=1, source_target_pairs={{0,64},{64,128},{128,192},{192,256},{256,320},{320,384},{384,448},... | collective-permute-start | bytes 983048 | tf_op jit(solution)/shard_map/ppermute | solution.py:65
  72.8 9.1 %collective-permute-start.5 = (bf16[256,640]{0,1:T(8,128)(2,1)S(1)}, bf16[256,640]{0,1:T(8,128)(2,1)S(1)}, u32[]{:S(2)}, u32[]{:S(2)}) collective-permute-start(bf16[256,640]{0,1:T(8,128)(2,1)S(1)} %collective-permute-done.4), channel_id=1, source_target_pairs={{0,64},{64,128},{128,192},{192,256},{256,320},{320,384},{384,448},... | collective-permute-start | bytes 983048 | tf_op jit(solution)/shard_map/ppermute | solution.py:65
  81.9 9.3 %collective-permute-start.6 = (bf16[256,640]{0,1:T(8,128)(2,1)S(1)}, bf16[256,640]{0,1:T(8,128)(2,1)S(1)}, u32[]{:S(2)}, u32[]{:S(2)}) collective-permute-start(bf16[256,640]{0,1:T(8,128)(2,1)S(1)} %collective-permute-done.5), channel_id=1, source_target_pairs={{0,64},{64,128},{128,192},{192,256},{256,320},{320,384},{384,448},... | collective-permute-start | bytes 983048 | tf_op jit(solution)/shard_map/ppermute | solution.py:65
  106.2 3.9 %copy-start.2 = (s32[20]{0:T(128)S(1)}, s32[20]{0:T(128)}, u32[]{:S(2)}) copy-start(s32[20]{0:T(128)} %param.10) | copy-start | bytes 244
Sparse Core Ops, SparseCore 0:
  10.7 89.4 all-gather.1
